TPU v7x, 32 devices: a whole 2x2x4 slice. The times are simulated.
32 devices in a mesh: groups: 2 (over y), ctx: 16 (over z, x, core).
Axes of the slice: x: 2, y: 2, z: 4, core: 2. Of those that a mesh axis runs over, the one named last changes fastest.
Arguments:
- queries: bfloat16 [64, 8192], P('groups'), parts along dimension 0, may hold values from -12 to 12
- keys: bfloat16 [32768, 1024], P(('groups', 'ctx')), parts along dimension 0, may hold values from -6 to 6
- values: bfloat16 [32768, 1024], P(('groups', 'ctx')), parts along dimension 0, may hold values from -6 to 6
- valid_len: int32 [32], P('groups'), parts along dimension 0, may hold values from 1 to 1024, 12288 in all
- row_counts: int32 [8], P('groups'), parts along dimension 0, may hold values from 1 to 8, 24 in all
- out_weight: bfloat16 [8192, 8192], P('ctx'), may hold values from -0.25 to 0.25
Outputs:
- attended: bfloat16 [64, 8192], P('groups', 'ctx'), parts along dimension 0
There are 2 independent parts, one for each index of `groups`. A program takes and returns all parts, laid end to end along the dimension named above; an argument that names none is the same for every part. Nothing has to cross between parts.
Inputs may be any that keep to these rules, and one draw needn't show every extreme that they name: `valid_len`: positions in use are the first ones of each shard; every shard uses at least one, and one shard uses all 1024. `row_counts`: the first rows of each batch are live, the others are padding; the counts sum to 24 and one batch is full.
All inputs are finite; a program needn't handle non-finite values.
Results may differ from a plain program's by a relative error of at most 0.0049.
Values may be sent and summed in bfloat16 or wider, within the bound.
A program may use at most 64 MiB of HBM per device.

v0:
```python
import functools
import math

import jax
import jax.numpy as jnp
from jax import lax
from jax.experimental import pallas as pl
from jax.experimental.pallas import tpu as pltpu
from jax.sharding import PartitionSpec as P

HEADS = 64
KVH = 8
HD = 128
BATCH_ROWS = 8
NBATCH = 4
LIVE_ROWS = 24


def on_device(queries, keys, values, valid_len, row_counts, out_weight):
    shards = lax.axis_size("ctx")
    my_index = lax.axis_index("ctx")
    ctx_rows = keys.shape[0]
    per_kv = HEADS // KVH
    head_width = per_kv * HD
    col_width = HEADS * HD // shards
    slot_width = max(HEADS, shards) // shards
    inv_root = 1.0 / math.sqrt(HD)
    own_count = jnp.sum(jnp.where(jnp.arange(shards, dtype=jnp.int32) == my_index, valid_len, 0))
    key_valid = jnp.arange(ctx_rows, dtype=jnp.int32) < own_count
    num_rows = queries.shape[0]
    outputs = []
    log_sums = []
    for kv_index in range(KVH):
        query_block = queries[:, kv_index * head_width : (kv_index + 1) * head_width].reshape(
            num_rows, per_kv, HD
        )
        key_block = keys[:, kv_index * HD : (kv_index + 1) * HD]
        value_block = values[:, kv_index * HD : (kv_index + 1) * HD]
        scores = (
            jnp.einsum("rgd,pd->rgp", query_block, key_block, preferred_element_type=jnp.float32)
            * inv_root
        )
        scores = jnp.where(key_valid, scores, -jnp.inf)
        peak = jnp.max(scores, axis=-1, keepdims=True)
        exp_scores = jnp.exp(scores - peak)
        expo_sum = jnp.sum(exp_scores, axis=-1)
        weights = exp_scores.astype(jnp.bfloat16)
        head_out = (
            jnp.einsum("rgp,pd->rgd", weights, value_block, preferred_element_type=jnp.float32)
            / expo_sum[..., None]
        )
        outputs.append(head_out.reshape(num_rows, head_width))
        log_sums.append(peak[..., 0] + jnp.log(expo_sum))
    partial_value, log_sums = (jnp.concatenate(outputs, axis=1), jnp.concatenate(log_sums, axis=1))
    slot_sums = jnp.repeat(log_sums, max(1, shards // HEADS), axis=1)
    combine_partial_value = lax.all_to_all(
        partial_value[None], "ctx", split_axis=2, concat_axis=0, tiled=True
    )
    combine_slot_sums = lax.all_to_all(
        slot_sums[None], "ctx", split_axis=2, concat_axis=0, tiled=True
    )
    biggest = jnp.max(combine_slot_sums, axis=0, keepdims=True)
    merge_wts = jnp.exp(combine_slot_sums - biggest)
    merge_sum = jnp.sum(merge_wts, axis=0)
    spread_wts = jnp.repeat(merge_wts, col_width // slot_width, axis=2)
    merged = jnp.sum(spread_wts * combine_partial_value, axis=0) / jnp.repeat(
        merge_sum, col_width // slot_width, axis=1
    )
    project_merged = merged.astype(jnp.bfloat16)
    term = jnp.dot(project_merged, out_weight, preferred_element_type=jnp.float32)
    projected = lax.psum_scatter(term, "ctx", scatter_dimension=1, tiled=True)
    row_ids = jnp.arange(queries.shape[0], dtype=jnp.int32)
    batch_ids = row_ids // BATCH_ROWS
    row_limit = jnp.sum(
        jnp.where(
            batch_ids[:, None] == jnp.arange(NBATCH, dtype=jnp.int32)[None, :],
            row_counts[None, :],
            0,
        ),
        axis=1,
    )
    live_rows = row_ids % BATCH_ROWS < row_limit
    return jnp.where(live_rows[:, None], projected, 0.0).astype(jnp.bfloat16)


def fused_kernel(
    shards,
    lens_hbm,
    counts_hbm,
    q_hbm,
    k_hbm,
    v_hbm,
    w_hbm,
    out_ref,
    lens_ref,
    counts_ref,
    q_s,
    k_s,
    v_s,
    w_s,
    num_own,
    stat_own,
    core_send,
    core_recv,
    core_stat_send,
    core_stat_recv,
    mid_send,
    mid_recv,
    mid_stat_send,
    mid_stat_recv,
    top_send,
    top_recv,
    top_stat_send,
    top_stat_recv,
    term_own,
    tcore_send,
    tcore_recv,
    tmid_send,
    tmid_recv,
    ttop_send,
    ttop_recv,
    int_sem,
    q_sem,
    k_sem,
    v_sem,
    w_sem,
    core_ss,
    core_rs,
    mid_ss,
    mid_rs,
    top_ss,
    top_rs,
    tcore_ss,
    tcore_rs,
    tmid_ss,
    tmid_rs,
    ttop_ss,
    ttop_rs,
):
    me = lax.axis_index("ctx")
    tops = shards // 4
    core, mid, top = me % 2, (me // 2) % 2, me // 4
    chips = 2 * tops
    num_rows = q_hbm.shape[0]
    half_heads = HEADS // KVH // 2
    half = half_heads * HD
    width = w_hbm.shape[1] // shards
    ctx_rows = k_hbm.shape[0]

    apart = list(range(tops - 1, 0, -1))
    order = [(1, d) for d in apart] + [(0, d) for d in apart] + [(1, 0), (0, 0)]

    def top_at(d):
        place = 0
        bit = 1
        while bit < tops:
            place = place + bit * ((top // bit + d // bit) % 2)
            bit *= 2
        return place

    def chip_of(i):
        flip, d = order[i]
        return top_at(d) * 2 + (mid + flip) % 2

    core_peer = me + 1 - 2 * core
    mid_peer = me + 2 - 4 * mid

    def top_peer(d):
        return top_at(d) * 4 + mid * 2 + core

    loads = []
    for i in range(chips):
        kv = chip_of(i)
        first = pl.multiple_of(kv * 2 * half + core * half, half)
        second = pl.multiple_of(kv * 2 * half + (1 - core) * half, half)
        cols = pl.ds(pl.multiple_of(kv * HD, HD), HD)
        loads.append(
            (
                pltpu.make_async_copy(q_hbm.at[:, pl.ds(first, half)], q_s.at[i, 0], q_sem.at[i, 0]),
                pltpu.make_async_copy(q_hbm.at[:, pl.ds(second, half)], q_s.at[i, 1], q_sem.at[i, 1]),
                pltpu.make_async_copy(k_hbm.at[:, cols], k_s.at[i], k_sem.at[i]),
                pltpu.make_async_copy(v_hbm.at[:, cols], v_s.at[i], v_sem.at[i]),
            )
        )
    ints = (
        pltpu.make_async_copy(lens_hbm, lens_ref, int_sem.at[0]),
        pltpu.make_async_copy(counts_hbm, counts_ref, int_sem.at[1]),
    )
    for copy in loads[0] + ints + loads[1]:
        copy.start()
    w_loads = []
    for i in range(chips):
        pair = []
        for side in range(2):
            owner = chip_of(i) * 2 + (1 - core if side == 0 else core)
            cols = pl.ds(pl.multiple_of(owner * width, width), width)
            pair.append(pltpu.make_async_copy(w_hbm.at[:, cols], w_s.at[i, side], w_sem.at[i, side]))
        w_loads.append(pair)
    barrier = pltpu.get_barrier_semaphore()
    peers = [core_peer, mid_peer] + [top_peer(d) for d in range(1, tops)]
    for peer in peers:
        pl.semaphore_signal(
            barrier, inc=1, device_id={"ctx": peer}, device_id_type=pl.DeviceIdType.MESH
        )

    def remote(src, dst, send_sem, recv_sem, peer):
        return pltpu.make_async_remote_copy(
            src_ref=src,
            dst_ref=dst,
            send_sem=send_sem,
            recv_sem=recv_sem,
            device_id={"ctx": peer},
            device_id_type=pl.DeviceIdType.MESH,
        )

    def merge_copies(kind, i, peer):
        send, recv, stat_send, stat_recv, ss, rs = kind
        return (
            remote(send.at[i], recv.at[i], ss.at[0, i], rs.at[0, i], peer),
            remote(stat_send.at[i], stat_recv.at[i], ss.at[1, i], rs.at[1, i], peer),
        )

    core_kind = (core_send, core_recv, core_stat_send, core_stat_recv, core_ss, core_rs)
    mid_kind = (mid_send, mid_recv, mid_stat_send, mid_stat_recv, mid_ss, mid_rs)
    top_kind = (top_send, top_recv, top_stat_send, top_stat_recv, top_ss, top_rs)
    sent = []

    gain = math.log2(math.e) / math.sqrt(HD)
    stat_row = lax.broadcasted_iota(jnp.int32, (8, 128), 0)

    def pack(peak, total):
        return jnp.where(stat_row < 4, peak, total)

    def join(parts):
        top_peak = functools.reduce(jnp.maximum, [p for _, p, _ in parts])
        num, total = None, None
        for n, p, t in parts:
            factor = jnp.exp2((p - top_peak) * gain)
            n, t = n * factor, t * factor
            num, total = (n, t) if num is None else (num + n, total + t)
        return num, top_peak, total

    def received(kind, i, peer):
        for copy in merge_copies(kind, i, peer):
            copy.wait_recv()
        return kind[1][i].astype(jnp.float32), kind[3][i, 0:1, :], kind[3][i, 4:5, :]

    def give(kind, i, peer, part):
        kind[0][i] = part[0].astype(kind[0].dtype)
        kind[2][i] = pack(part[1], part[2])
        for copy in merge_copies(kind, i, peer):
            copy.start()
            sent.append(copy)

    def ready(i):
        for copy in loads[i]:
            copy.wait()
        for copy in w_loads[i] if i + 2 >= chips else list(loads[i + 2]) + w_loads[i]:
            copy.start()
        if i == 0:
            for copy in ints:
                copy.wait()

    def scores_of(i):
        q = jnp.concatenate(
            [q_s[i, side, :, g * HD : (g + 1) * HD] for side in range(2) for g in range(half_heads)],
            axis=0,
        )
        return lax.dot_general(
            k_s[i], q, (((1,), (1,)), ((), ())), preferred_element_type=jnp.float32
        )

    def attend(i, scores):
        if i + 1 < chips:
            ready(i + 1)
        own_count = lens_ref[me]
        later = scores_of(i + 1) if i + 1 < chips else None
        pos = lax.broadcasted_iota(jnp.int32, scores.shape, 0)
        scores = jnp.where(pos < own_count, scores, -jnp.inf)
        peak = jnp.max(scores, axis=0, keepdims=True)
        expo = jnp.exp2((scores - peak) * gain)
        total = jnp.sum(expo, axis=0, keepdims=True)
        num = lax.dot_general(
            v_s[i],
            expo.astype(jnp.bfloat16),
            (((0,), (0,)), ((), ())),
            preferred_element_type=jnp.float32,
        )
        cut = half_heads * num_rows
        num_own[i] = num[:, :cut]
        stat_own[i] = pack(peak[:, :cut], total[:, :cut])
        if i == 0:
            pl.semaphore_wait(barrier, len(peers))
        give(core_kind, i, core_peer, (num[:, cut:], peak[:, cut:], total[:, cut:]))
        return later

    def own_part(i):
        return num_own[i], stat_own[i, 0:1, :], stat_own[i, 4:5, :]

    def settle(i):
        flip, d = order[i]
        part = join([own_part(i), received(core_kind, i, core_peer)])
        slot = d
        if flip:
            give(mid_kind, slot, mid_peer, part)
            return None
        part = join([part, received(mid_kind, slot, mid_peer)])
        if d:
            give(top_kind, d - 1, top_peer(d), part)
            return None
        return part

    ready(0)
    scores = scores_of(0)
    for i in range(chips):
        scores = attend(i, scores)
        if i:
            settle(i - 1)
    part = settle(chips - 1)
    part = join([part] + [received(top_kind, d - 1, top_peer(d)) for d in range(1, tops)])
    merged_t = part[0] / part[2]
    merged = jnp.transpose(merged_t)
    merged = jnp.concatenate(
        [merged[h * num_rows : (h + 1) * num_rows] for h in range(half_heads)], axis=1
    ).astype(jnp.bfloat16)

    def picks(shape, row_axis):
        row = lax.broadcasted_iota(jnp.int32, shape, row_axis)
        place = lax.broadcasted_iota(jnp.int32, shape, 1 - row_axis)
        before, seat = jnp.int32(0), jnp.full(shape, -1, jnp.int32)
        for b in range(NBATCH):
            count = counts_ref[b]
            inside = row - b * BATCH_ROWS
            here = jnp.logical_and(inside >= 0, jnp.logical_and(inside < BATCH_ROWS, inside < count))
            seat = jnp.where(here, before + inside, seat)
            before = before + count
        return jnp.where(seat == place, 1.0, 0.0).astype(jnp.bfloat16)

    merged = jnp.dot(
        picks((LIVE_ROWS, num_rows), 1), merged, preferred_element_type=jnp.float32
    ).astype(jnp.bfloat16)

    def term(i, side):
        w_loads[i][side].wait()
        return jnp.dot(merged, w_s[i, side], preferred_element_type=jnp.float32)

    def term_copy(kind, i, peer):
        send, recv, ss, rs = kind
        return remote(send.at[i], recv.at[i], ss.at[i], rs.at[i], peer)

    tcore_kind = (tcore_send, tcore_recv, tcore_ss, tcore_rs)
    tmid_kind = (tmid_send, tmid_recv, tmid_ss, tmid_rs)
    ttop_kind = (ttop_send, ttop_recv, ttop_ss, ttop_rs)

    def give_term(kind, i, peer, value):
        kind[0][i] = value.astype(jnp.bfloat16)
        copy = term_copy(kind, i, peer)
        copy.start()
        sent.append(copy)

    def received_term(kind, i, peer):
        term_copy(kind, i, peer).wait_recv()
        return kind[1][i].astype(jnp.float32)

    def settle_term(i):
        flip, d = order[i]
        value = term_own[i] + received_term(tcore_kind, i, core_peer)
        slot = d
        if flip:
            give_term(tmid_kind, slot, mid_peer, value)
            return None
        value = value + received_term(tmid_kind, slot, mid_peer)
        if d:
            give_term(ttop_kind, d - 1, top_peer(d), value)
            return None
        return value

    for i in range(chips):
        give_term(tcore_kind, i, core_peer, term(i, 0))
        term_own[i] = term(i, 1)
        if i >= 2:
            settle_term(i - 2)
    settle_term(chips - 2)
    value = settle_term(chips - 1)
    for d in range(1, tops):
        value = value + received_term(ttop_kind, d - 1, top_peer(d))
    out_ref[...] = jnp.dot(
        picks((num_rows, LIVE_ROWS), 0),
        value.astype(jnp.bfloat16),
        preferred_element_type=jnp.float32,
    ).astype(out_ref.dtype)
    for copy in sent:
        copy.wait_send()


def fused_on_device(shards, queries, keys, values, valid_len, row_counts, out_weight):
    num_rows = queries.shape[0]
    ctx_rows = keys.shape[0]
    chips = shards // 2
    tops = shards // 4
    half = HEADS // KVH // 2 * HD
    cut = HEADS // KVH // 2 * num_rows
    depth, width = out_weight.shape[0], out_weight.shape[1] // shards
    vmem = pltpu.VMEM
    bf16, f32 = jnp.bfloat16, jnp.float32

    def merge_slots(count, kind=bf16):
        return [
            vmem((count, HD, cut), kind),
            vmem((count, HD, cut), kind),
            vmem((count, 8, cut), f32),
            vmem((count, 8, cut), f32),
        ]

    def term_slots(count):
        return [vmem((count, LIVE_ROWS, width), bf16)] * 2

    dma = pltpu.SemaphoreType.DMA
    return pl.pallas_call(
        functools.partial(fused_kernel, shards),
        out_shape=jax.ShapeDtypeStruct((num_rows, width), bf16),
        in_specs=[pl.BlockSpec(memory_space=pl.ANY)] * 6,
        out_specs=pl.BlockSpec(memory_space=pltpu.VMEM),
        scratch_shapes=[
            pltpu.SMEM(valid_len.shape, jnp.int32),
            pltpu.SMEM(row_counts.shape, jnp.int32),
            vmem((chips, 2, num_rows, half), bf16),
            vmem((chips, ctx_rows, HD), bf16),
            vmem((chips, ctx_rows, HD), bf16),
            vmem((chips, 2, depth, width), bf16),
            vmem((chips, HD, cut), f32),
            vmem((chips, 8, cut), f32),
        ]
        + merge_slots(chips, f32)
        + merge_slots(tops)
        + merge_slots(tops - 1)
        + [vmem((chips, LIVE_ROWS, width), f32)]
        + term_slots(chips)
        + term_slots(tops)
        + term_slots(tops - 1)
        + [dma((2,)), dma((chips, 2)), dma((chips,)), dma((chips,)), dma((chips, 2))]
        + [dma((2, chips))] * 2
        + [dma((2, tops))] * 2
        + [dma((2, tops - 1))] * 2
        + [dma((chips,))] * 2
        + [dma((tops,))] * 2
        + [dma((tops - 1,))] * 2,
        compiler_params=pltpu.CompilerParams(
            collective_id=0, has_side_effects=True, vmem_limit_bytes=60 << 20
        ),
    )(valid_len, row_counts, queries, keys, values, out_weight)


def solution(mesh):
    shards = mesh.shape["ctx"]
    body = functools.partial(fused_on_device, shards) if shards == 2 * KVH else on_device
    return jax.shard_map(
        body,
        mesh=mesh,
        in_specs=(
            P("groups", None),
            P(("groups", "ctx"), None),
            P(("groups", "ctx"), None),
            P("groups"),
            P("groups"),
            P("ctx", None),
        ),
        out_specs=P("groups", "ctx"),
        check_vma=False,
    )
```

profile of v0, /device:TPU:0, one launch (start us, length us, event | category | flops | bytes accessed | tf_op | source)
XLA Modules:
  0.0 26.6 jit_solution(12061887341606624845)
XLA Ops:
  0.0 25.2 %shard_map.64 = bf16[32,512]{1,0:T(8,128)(2,1)} custom-call(s32[16]{0:T(128)} %lens_hbm.1, s32[4]{0:T(128)} %counts_hbm.1, bf16[32,8192]{1,0:T(8,128)(2,1)} %q_hbm.1, bf16[1024,1024]{1,0:T(8,128)(2,1)} %k_hbm.1, bf16[1024,1024]{1,0:T(8,128)(2,1)} %v_hbm.1, bf16[512,8192]{1,0:T(8,128)(2,1)} %w_hbm.1), custom_call_target="tpu_custom_call" | custom-call | tf_op jit(solution)/shard_map/pallas_call | solution.py:419
  25.2 1.4 %copy.8 = bf16[32,512]{1,0:T(8,128)(2,1)} copy(bf16[32,512]{1,0:T(8,128)(2,1)} %shard_map.64) | data formatting | bytes 65536
where the time goes:
time: 26.8 us; the launch traced here: 26.6 us
  Pallas kernels  25.2 us (94%)
  local copies, waits for them, and re-layouts  1.38 us (5%)
    pallas_call x1, Pallas kernels, fused_on_device(): pl.pallas_call(functools.partial(fused_kernel, shards), out_shape=jax.Sha...  25.2 us
    unnamed x1, local copies, waits for them, and re-layouts  1.38 us

commit v1 on v0

--- a/solution.py
+++ b/solution.py
@@ -418,7 +418,7 @@
     dma = pltpu.SemaphoreType.DMA
     return pl.pallas_call(
         functools.partial(fused_kernel, shards),
-        out_shape=jax.ShapeDtypeStruct((num_rows, width), bf16),
+        out_shape=pltpu.VMEM((num_rows, width), bf16),
         in_specs=[pl.BlockSpec(memory_space=pl.ANY)] * 6,
         out_specs=pl.BlockSpec(memory_space=pltpu.VMEM),
         scratch_shapes=[

time: 26.8 us -> 25.4 us (0.948)
  local copies, waits for them, and re-layouts: 1.38 us -> 0.62 us
  Pallas kernels: 25.2 us -> 24.6 us
    unnamed x1, local copies, waits for them, and re-layouts: 1.38 us -> 0.62 us
    pallas_call x1, Pallas kernels: 25.2 us -> 24.6 us  [fused_on_device(): pl.pallas_call(functools.partial(fused_kernel, shards), out_shape=pltpu.V...]
where the time goes in v1:
time: 25.4 us; the launch traced here: 25.2 us
  Pallas kernels  24.6 us (97%)
  local copies, waits for them, and re-layouts  0.62 us (2%)
    pallas_call x1, Pallas kernels, fused_on_device(): pl.pallas_call(functools.partial(fused_kernel, shards), out_shape=pltpu.V...  24.6 us
    unnamed x1, local copies, waits for them, and re-layouts  0.62 us

profile of v1, /device:TPU:0, one launch (start us, length us, event | category | flops | bytes accessed | tf_op | source)
XLA Modules:
  0.0 25.2 jit_solution(14993630359575836870)
XLA Ops:
  0.0 24.6 %shard_map.64 = bf16[32,512]{1,0:T(8,128)(2,1)S(1)} custom-call(s32[16]{0:T(128)} %lens_hbm.1, s32[4]{0:T(128)} %counts_hbm.1, bf16[32,8192]{1,0:T(8,128)(2,1)} %q_hbm.1, bf16[1024,1024]{1,0:T(8,128)(2,1)} %k_hbm.1, bf16[1024,1024]{1,0:T(8,128)(2,1)} %v_hbm.1, bf16[512,8192]{1,0:T(8,128)(2,1)} %w_hbm.1), custom_call_target="tpu_custom_call" | custom-call | tf_op jit(solution)/shard_map/pallas_call | solution.py:419
  24.6 0.6 %copy.8 = bf16[32,512]{1,0:T(8,128)(2,1)} copy(bf16[32,512]{1,0:T(8,128)(2,1)S(1)} %shard_map.64) | data formatting | bytes 65536
